TPU v7x, 32 devices: a whole 2x2x4 slice. The times are simulated.
32 devices in a mesh: tm: 8 (over z, y), space: 4 (over x, core).
Axes of the slice: x: 2, y: 2, z: 4, core: 2. Of those that a mesh axis runs over, the one named last changes fastest.
Arguments:
- controls: bfloat16 [32, 64, 2048], P('tm', None, 'space'), may hold values from -4 to 4
- target: bfloat16 [64, 2048], P(None, 'space'), may hold values from -4 to 4
- state_in: float32 [8, 64, 2048], P('tm', None, 'space'), may hold values from -2.5 to 2.5
- adjoint_in: float32 [8, 64, 2048], P('tm', None, 'space'), may hold values from -5 to 5
- block_inverse: bfloat16 [64, 64, 2048], P(None, None, 'space'), may hold values from -1 to 1
- numbering: int32 [4, 512], P('space'), may hold values from 0 to 511, each once within a row
Outputs:
- new_controls: bfloat16 [32, 64, 2048], P('tm', None, 'space')
- next_state: float32 [8, 64, 2048], P('tm', None, 'space')
- next_adjoint: float32 [8, 64, 2048], P('tm', None, 'space')
- objective: float32 [], replicated
Inputs may be any that keep to these rules, and one draw needn't show every extreme that they name: `numbering`: each row names every structural element of its slab exactly once.
All inputs are finite; a program needn't handle non-finite values.
Results may differ from a plain program's by a relative error of at most 0.0085.
Values may be sent and summed in bfloat16 or wider, within the bound.
A program may use at most 128 MiB of HBM per device.

v0:
```python
import jax
import jax.numpy as jnp
from jax import lax
from jax.sharding import PartitionSpec as P

NSIDE = 4
EXY = 16
TIME_STEP = 0.1
PENALTY = 0.5
REGULAR = 0.1


def padded_2(cells, sides, width):
    for axis, dim in sides:
        count = lax.axis_size(axis)
        ends = count - 1
        head = lax.slice_in_dim(cells, 0, width, axis=dim)
        tail = lax.slice_in_dim(cells, cells.shape[dim] - width, cells.shape[dim], axis=dim)
        cells = jnp.concatenate(
            [
                lax.ppermute(tail, axis, [(i, (i + 1) % count) for i in range(ends)]),
                cells,
                lax.ppermute(head, axis, [((i + 1) % count, i) for i in range(ends)]),
            ],
            axis=dim,
        )
    return cells


def from_behind(shard, axis, by):
    length = lax.axis_size(axis)
    pairs = [(i, i + by) for i in range(length) if 0 <= i + by < length]
    return lax.ppermute(shard, axis, pairs)


def apply_block(blocks, right_side):
    return jnp.einsum("ije,je->ie", blocks, right_side, preferred_element_type=jnp.float32)


def apply_transpose(blocks, vector):
    return jnp.einsum("ije,ie->je", blocks, vector, preferred_element_type=jnp.float32)


def face_jumps(values, fetch, edges, node_side, elements):
    tensor = values.reshape(node_side, node_side, node_side, elements)
    last = node_side - 1
    lower_rim, upper_rim = edges(tensor[0], tensor[last])
    padded = padded_2(
        jnp.stack([lower_rim, upper_rim]).astype(jnp.bfloat16), (("space", 0),), 1
    ).astype(jnp.float32)
    rims = (padded[0], padded[3])
    west_jump = fetch("west", tensor[:, :, last, :], rims) - tensor[:, :, 0, :]
    east_jump = fetch("east", tensor[:, :, 0, :], rims) - tensor[:, :, last, :]
    south_jump = fetch("south", tensor[:, last, :, :], rims) - tensor[:, 0, :, :]
    north_jump = fetch("north", tensor[:, 0, :, :], rims) - tensor[:, last, :, :]
    lower_jump = fetch("lower", tensor[last], rims) - tensor[0]
    upper_jump = fetch("upper", tensor[0], rims) - tensor[last]
    total = jnp.zeros_like(tensor)
    total = total.at[:, :, 0, :].add(west_jump)
    total = total.at[:, :, last, :].add(east_jump)
    total = total.at[:, 0, :, :].add(south_jump)
    total = total.at[:, last, :, :].add(north_jump)
    total = total.at[0].add(lower_jump)
    total = total.at[last].add(upper_jump)
    return total.reshape(values.shape)


def per_device(controls, target, state_in, adjoint_in, block_inverse, numbering):
    steps_here = controls.shape[0]
    nodes = controls.shape[1]
    elements = controls.shape[2]
    node_side = NSIDE
    layer_cells = EXY * EXY
    layers = elements // layer_cells
    ordering = numbering[0]
    position = jnp.arange(elements, dtype=jnp.int32)
    inverse = jnp.zeros((elements,), jnp.int32).at[ordering].set(position)

    def arrange(values):
        return jnp.take(values, inverse, axis=-1)

    def restore(values):
        return jnp.take(values, ordering, axis=-1)

    def edges(lower_face, upper_face):
        return (lower_face[:, :, :layer_cells], upper_face[:, :, elements - layer_cells :])

    def fetch(face_name, traces, rims):
        shaped = traces.reshape(node_side, node_side, layers, EXY, EXY)
        if face_name == "west":
            moved = jnp.roll(shaped, 1, axis=4)
        elif face_name == "east":
            moved = jnp.roll(shaped, -1, axis=4)
        elif face_name == "south":
            moved = jnp.roll(shaped, 1, axis=3)
        elif face_name == "north":
            moved = jnp.roll(shaped, -1, axis=3)
        elif face_name == "lower":
            remote = rims[0].reshape(node_side, node_side, 1, EXY, EXY)
            moved = jnp.concatenate([remote, shaped[:, :, :-1]], axis=2)
        else:
            remote = rims[1].reshape(node_side, node_side, 1, EXY, EXY)
            moved = jnp.concatenate([shaped[:, :, 1:], remote], axis=2)
        return moved.reshape(traces.shape)

    def jumps_of(values):
        return face_jumps(values, fetch, edges, node_side, elements)

    blocks = arrange(block_inverse)
    goal = arrange(target).astype(jnp.float32)
    controls_here = arrange(controls)
    start_state = arrange(state_in[0])
    start_adjoint = arrange(adjoint_in[0])
    total_steps = steps_here * lax.axis_size("tm")
    first_step = lax.axis_index("tm") * steps_here
    history = [start_state]
    state = start_state
    misfit = jnp.float32(0.0)
    regular_sum = jnp.float32(0.0)
    right_side = None
    for index_k in range(steps_here):
        control_now = controls_here[index_k].astype(jnp.float32)
        right_side = (
            state
            + TIME_STEP * (state - state * state * state)
            + TIME_STEP * PENALTY * jumps_of(state)
            + TIME_STEP * control_now
        ).astype(jnp.bfloat16)
        state = apply_block(blocks, right_side)
        history.append(state)
        weight = (first_step + index_k + 1).astype(jnp.float32) / total_steps
        misfit = misfit + weight * jnp.sum((state - goal) ** 2)
        regular_sum = regular_sum + jnp.sum(control_now * control_now)
    local_cost = 0.5 * misfit + 0.5 * REGULAR * regular_sum
    end_weight = (first_step + steps_here).astype(jnp.float32) / total_steps
    adjoint = end_weight * (history[-1] - goal) + start_adjoint
    updated = [None] * steps_here
    carried = adjoint
    for index_k in reversed(range(steps_here)):
        pulled = apply_transpose(blocks, adjoint.astype(jnp.bfloat16))
        control_now = controls_here[index_k].astype(jnp.float32)
        updated[index_k] = (control_now - (TIME_STEP * pulled + REGULAR * control_now)).astype(
            jnp.bfloat16
        )
        before = history[index_k]
        carried = (
            pulled
            + TIME_STEP * (1.0 - 3.0 * before * before) * pulled
            + TIME_STEP * PENALTY * jumps_of(pulled)
        )
        if index_k > 0:
            weight = (first_step + index_k).astype(jnp.float32) / total_steps
            adjoint = weight * (before - goal) + carried
    new_controls = restore(jnp.stack(updated))
    objective = lax.psum(local_cost, ("tm", "space")) / (
        total_steps * nodes * elements * lax.axis_size("space")
    )
    moved_state = from_behind(history[-1].astype(jnp.bfloat16), "tm", 1).astype(jnp.float32)
    next_state = jnp.where(lax.axis_index("tm") == 0, state_in[0], restore(moved_state))[None]
    next_adjoint = from_behind(restore(carried), "tm", -1)[None]
    return (new_controls, next_state, next_adjoint, objective)


def solution(mesh):
    return jax.shard_map(
        per_device,
        mesh=mesh,
        in_specs=(
            P("tm", None, "space"),
            P(None, "space"),
            P("tm", None, "space"),
            P("tm", None, "space"),
            P(None, None, "space"),
            P("space", None),
        ),
        out_specs=(P("tm", None, "space"), P("tm", None, "space"), P("tm", None, "space"), P()),
        check_vma=False,
    )
```

profile of v0, /device:TPU:0, one launch (start us, length us, event | category | flops | bytes accessed | tf_op | source)
XLA Modules:
  0.0 264.8 jit_solution(15748085955801050513)
XLA Ops:
  1.4 2.4 scatter_custom_fusion
  6.1 2.4 collective-permute-start
  15.7 13.0 %copy.148 = bf16[64,64,512]{1,0,2:T(8,128)(2,1)} copy(bf16[64,64,512]{2,1,0:T(8,128)(2,1)} %param.110) | data formatting | bytes 8388608 | tf_op args[4]
  28.8 23.0 %gather_fusion = bf16[512,64,64]{2,1,0:T(8,128)(2,1)} fusion(bf16[64,64,512]{1,0,2:T(8,128)(2,1)} %copy.148, s32[1024]{0:T(1024)S(1)} %pad_clamp_fusion.1), kind=kCustom, calls=%fused_computation.6 | custom fusion | bytes 8390656 | tf_op jit(solution)/shard_map/jit(_take)/gather | solution.py:80
  55.7 8.3 %fusion = f32[512,64]{1,0:T(8,128)S(1)} fusion(f32[512,64]{1,0:T(8,128)S(1)} %copy.235, bf16[512,64,64]{2,1,0:T(8,128)(2,1)} %gather_fusion, pred[512]{0:T(512)(128)(4,1)S(1)} %compare_and_fusion.1), kind=kLoop, calls=%fused_computation.17 | loop fusion | flops 8355840 | bytes 4456960
  66.5 5.1 %collective-permute-start.2 = (bf16[1,4,4,256]{3,2,1,0:T(4,128)(2,1)S(1)}, bf16[1,4,4,256]{3,2,1,0:T(4,128)(2,1)S(1)}, u32[]{:S(2)}, u32[]{:S(2)}) collective-permute-start(bf16[1,4,4,256]{3,2,1,0:T(4,128)(2,1)S(1)} %slice_bitcast_fusion.17), channel_id=1, source_target_pairs={{0,1},{1,2},{2,3},{4,5},{5,6},{6,7},{8,9},{9,10},{10,11},{12,13},{... | collective-permute-start | bytes 24584 | tf_op jit(solution)/shard_map/ppermute | solution.py:21
  73.5 2.4 collective-permute-done.3
  76.9 8.1 %fusion.1 = f32[512,64]{1,0:T(8,128)S(1)} fusion(f32[512,64]{1,0:T(8,128)S(1)} %copy.236, bf16[512,64,64]{2,1,0:T(8,128)(2,1)} %gather_fusion, pred[512]{0:T(512)(128)(4,1)S(1)} %compare_and_fusion.1), kind=kLoop, calls=%fused_computation.18 | loop fusion | flops 8355840 | bytes 4456960
  87.5 4.3 %collective-permute-start.4 = (bf16[1,4,4,256]{3,2,1,0:T(4,128)(2,1)S(1)}, bf16[1,4,4,256]{3,2,1,0:T(4,128)(2,1)S(1)}, u32[]{:S(2)}, u32[]{:S(2)}) collective-permute-start(bf16[1,4,4,256]{3,2,1,0:T(4,128)(2,1)S(1)} %slice_bitcast_fusion.15), channel_id=1, source_target_pairs={{0,1},{1,2},{2,3},{4,5},{5,6},{6,7},{8,9},{9,10},{10,11},{12,13},{... | collective-permute-start | bytes 24584 | tf_op jit(solution)/shard_map/ppermute | solution.py:21
  95.8 8.5 %fusion.2 = f32[512,64]{1,0:T(8,128)S(1)} fusion(f32[512,64]{1,0:T(8,128)S(1)} %copy.237, bf16[512,64,64]{2,1,0:T(8,128)(2,1)} %gather_fusion, pred[512]{0:T(512)(128)(4,1)S(1)} %compare_and_fusion.1), kind=kLoop, calls=%fused_computation.19 | loop fusion | flops 8355840 | bytes 4456960
  106.8 3.8 %collective-permute-start.6 = (bf16[1,4,4,256]{3,2,1,0:T(4,128)(2,1)S(1)}, bf16[1,4,4,256]{3,2,1,0:T(4,128)(2,1)S(1)}, u32[]{:S(2)}, u32[]{:S(2)}) collective-permute-start(bf16[1,4,4,256]{3,2,1,0:T(4,128)(2,1)S(1)} %slice_bitcast_fusion.13), channel_id=1, source_target_pairs={{0,1},{1,2},{2,3},{4,5},{5,6},{6,7},{8,9},{9,10},{10,11},{12,13},{... | collective-permute-start | bytes 24584 | tf_op jit(solution)/shard_map/ppermute | solution.py:21
  114.7 8.1 %fusion.3 = f32[512,64]{1,0:T(8,128)S(1)} fusion(f32[512,64]{1,0:T(8,128)S(1)} %copy.238, bf16[512,64,64]{2,1,0:T(8,128)(2,1)} %gather_fusion, pred[512]{0:T(512)(128)(4,1)S(1)} %compare_and_fusion.1), kind=kLoop, calls=%fused_computation.20 | loop fusion | flops 8355840 | bytes 4456960
  123.1 8.2 %fusion.4 = f32[512,64]{1,0:T(8,128)S(1)} fusion(f32[512,64]{1,0:T(8,128)S(1)} %copy.239, bf16[512,64,64]{2,1,0:T(8,128)(2,1)} %gather_fusion, pred[512]{0:T(512)(128)(4,1)S(1)} %compare_and_fusion.1), kind=kLoop, calls=%fused_computation.21 | loop fusion | flops 8355840 | bytes 4456960
  134.0 3.8 %collective-permute-start.8 = (bf16[1,4,4,256]{3,2,1,0:T(4,128)(2,1)S(1)}, bf16[1,4,4,256]{3,2,1,0:T(4,128)(2,1)S(1)}, u32[]{:S(2)}, u32[]{:S(2)}) collective-permute-start(bf16[1,4,4,256]{3,2,1,0:T(4,128)(2,1)S(1)} %slice_bitcast_fusion.11), channel_id=1, source_target_pairs={{0,1},{1,2},{2,3},{4,5},{5,6},{6,7},{8,9},{9,10},{10,11},{12,13},{... | collective-permute-start | bytes 24584 | tf_op jit(solution)/shard_map/ppermute | solution.py:21
  139.4 3.4 %collective-permute-start.14 = (bf16[64,512]{1,0:T(8,128)(2,1)S(1)}, bf16[64,512]{1,0:T(8,128)(2,1)S(1)}, u32[]{:S(2)}, u32[]{:S(2)}) collective-permute-start(bf16[64,512]{1,0:T(8,128)(2,1)S(1)} %bitcast_convert_fusion), channel_id=1, source_target_pairs={{0,4},{4,8},{8,12},{12,16},{16,20},{20,24},{24,28},{1,5},{5,9},{9,... | collective-permute-start | bytes 196616 | tf_op jit(solution)/shard_map/ppermute | solution.py:33
  144.0 8.4 %fusion.5 = f32[512,64]{1,0:T(8,128)S(1)} fusion(f32[512,64]{1,0:T(8,128)S(1)} %copy.240, bf16[512,64,64]{2,1,0:T(8,128)(2,1)} %gather_fusion, pred[512]{0:T(512)(128)(4,1)S(1)} %compare_and_fusion.1), kind=kLoop, calls=%fused_computation.22 | loop fusion | flops 8355840 | bytes 4456960
  154.8 2.8 %collective-permute-start.10 = (bf16[1,4,4,256]{3,2,1,0:T(4,128)(2,1)S(1)}, bf16[1,4,4,256]{3,2,1,0:T(4,128)(2,1)S(1)}, u32[]{:S(2)}, u32[]{:S(2)}) collective-permute-start(bf16[1,4,4,256]{3,2,1,0:T(4,128)(2,1)S(1)} %slice_bitcast_fusion.9), channel_id=1, source_target_pairs={{0,1},{1,2},{2,3},{4,5},{5,6},{6,7},{8,9},{9,10},{10,11},{12,13},{... | collective-permute-start | bytes 24584 | tf_op jit(solution)/shard_map/ppermute | solution.py:21
  159.5 2.2 collective-permute-done.11
  163.3 8.2 %fusion.6 = f32[512,64]{1,0:T(8,128)S(1)} fusion(f32[512,64]{1,0:T(8,128)S(1)} %copy.241, bf16[512,64,64]{2,1,0:T(8,128)(2,1)} %gather_fusion, pred[512]{0:T(512)(128)(4,1)S(1)} %compare_and_fusion.1), kind=kLoop, calls=%fused_computation.23 | loop fusion | flops 8355840 | bytes 4456960
  174.0 4.3 %collective-permute-start.12 = (bf16[1,4,4,256]{3,2,1,0:T(4,128)(2,1)S(1)}, bf16[1,4,4,256]{3,2,1,0:T(4,128)(2,1)S(1)}, u32[]{:S(2)}, u32[]{:S(2)}) collective-permute-start(bf16[1,4,4,256]{3,2,1,0:T(4,128)(2,1)S(1)} %slice_bitcast_fusion.7), channel_id=1, source_target_pairs={{0,1},{1,2},{2,3},{4,5},{5,6},{6,7},{8,9},{9,10},{10,11},{12,13},{... | collective-permute-start | bytes 24584 | tf_op jit(solution)/shard_map/ppermute | solution.py:21
  183.8 8.2 %fusion.7 = f32[512,64]{1,0:T(8,128)S(1)} fusion(f32[512,64]{1,0:T(8,128)S(1)} %copy.242, bf16[512,64,64]{2,1,0:T(8,128)(2,1)} %gather_fusion, pred[512]{0:T(512)(128)(4,1)S(1)} %compare_and_fusion.1), kind=kLoop, calls=%fused_computation.24 | loop fusion | flops 8355840 | bytes 4456960
  194.5 3.0 %collective-permute-start.15 = (bf16[1,4,4,256]{3,2,1,0:T(4,128)(2,1)S(1)}, bf16[1,4,4,256]{3,2,1,0:T(4,128)(2,1)S(1)}, u32[]{:S(2)}, u32[]{:S(2)}) collective-permute-start(bf16[1,4,4,256]{3,2,1,0:T(4,128)(2,1)S(1)} %slice_bitcast_fusion.5), channel_id=1, source_target_pairs={{0,1},{1,2},{2,3},{4,5},{5,6},{6,7},{8,9},{9,10},{10,11},{12,13},{... | collective-permute-start | bytes 24584 | tf_op jit(solution)/shard_map/ppermute | solution.py:21
  211.0 41.3 %psum.7 = f32[]{:T(128)} all-reduce(f32[]{:T(128)S(6)} %add.563), channel_id=1, replica_groups=mesh['tm'=8,'space'=4] {'tm','space'}, use_global_device_ids=true, to_apply=%region_9.12 | all-reduce | flops 1 | bytes 8 | tf_op jit(solution)/shard_map/psum | solution.py:155
  257.3 5.3 %collective-permute-done.17 = f32[64,512]{0,1:T(8,128)S(1)} collective-permute-done((f32[64,512]{0,1:T(8,128)S(1)}, f32[64,512]{0,1:T(8,128)S(1)}, u32[]{:S(2)}, u32[]{:S(2)}) %collective-permute-start.17) | collective-permute-done | bytes 131104 | tf_op jit(solution)/shard_map/ppermute | solution.py:33
  (477 shorter events, 64.8 us)
Async XLA Ops:
  0.6 11.7 %copy-start.3 = (s32[1,512]{1,0:T(1,128)S(1)}, s32[1,512]{1,0:T(1,128)}, u32[]{:S(2)}) copy-start(s32[1,512]{1,0:T(1,128)} %param.111) | copy-start | bytes 6148
  0.6 11.9 %copy-start = (bf16[4,64,512]{2,1,0:T(8,128)(2,1)S(1)}, bf16[4,64,512]{2,1,0:T(8,128)(2,1)}, u32[]{:S(2)}) copy-start(bf16[4,64,512]{2,1,0:T(8,128)(2,1)} %param.106) | copy-start | bytes 786436
  6.1 48.6 %collective-permute-start = (bf16[1,4,4,256]{3,2,1,0:T(4,128)(2,1)S(1)}, bf16[1,4,4,256]{3,2,1,0:T(4,128)(2,1)S(1)}, u32[]{:S(2)}, u32[]{:S(2)}) collective-permute-start(bf16[1,4,4,256]{3,2,1,0:T(4,128)(2,1)S(1)} %slice_bitcast_fusion.19), channel_id=1, source_target_pairs={{0,1},{1,2},{2,3},{4,5},{5,6},{6,7},{8,9},{9,10},{10,11},{12,13},{... | collective-permute-start | bytes 24584 | tf_op jit(solution)/shard_map/ppermute | solution.py:21
  8.6 46.2 %collective-permute-start.1 = (bf16[1,4,4,256]{3,2,1,0:T(4,128)(2,1)S(1)}, bf16[1,4,4,256]{3,2,1,0:T(4,128)(2,1)S(1)}, u32[]{:S(2)}, u32[]{:S(2)}) collective-permute-start(bf16[1,4,4,256]{3,2,1,0:T(4,128)(2,1)S(1)} %slice_bitcast_fusion.18), channel_id=1, source_target_pairs={{1,0},{2,1},{3,2},{5,4},{6,5},{7,6},{9,8},{10,9},{11,10},{13,12},{... | collective-permute-start | bytes 24584 | tf_op jit(solution)/shard_map/ppermute | solution.py:23
  15.7 36.1 %copy-start.2 = (bf16[64,512]{1,0:T(8,128)(2,1)S(1)}, bf16[64,512]{1,0:T(8,128)(2,1)}, u32[]{:S(2)}) copy-start(bf16[64,512]{1,0:T(8,128)(2,1)} %param.107) | copy-start | bytes 196612
  15.7 37.7 %copy-start.1 = (f32[1,64,512]{2,1,0:T(8,128)S(1)}, f32[1,64,512]{2,1,0:T(8,128)}, u32[]{:S(2)}) copy-start(f32[1,64,512]{2,1,0:T(8,128)} %param.109) | copy-start | bytes 393220
  66.5 7.1 %collective-permute-start.2 = (bf16[1,4,4,256]{3,2,1,0:T(4,128)(2,1)S(1)}, bf16[1,4,4,256]{3,2,1,0:T(4,128)(2,1)S(1)}, u32[]{:S(2)}, u32[]{:S(2)}) collective-permute-start(bf16[1,4,4,256]{3,2,1,0:T(4,128)(2,1)S(1)} %slice_bitcast_fusion.17), channel_id=1, source_target_pairs={{0,1},{1,2},{2,3},{4,5},{5,6},{6,7},{8,9},{9,10},{10,11},{12,13},{... | collective-permute-start | bytes 24584 | tf_op jit(solution)/shard_map/ppermute | solution.py:21
  71.6 4.3 %collective-permute-start.3 = (bf16[1,4,4,256]{3,2,1,0:T(4,128)(2,1)S(1)}, bf16[1,4,4,256]{3,2,1,0:T(4,128)(2,1)S(1)}, u32[]{:S(2)}, u32[]{:S(2)}) collective-permute-start(bf16[1,4,4,256]{3,2,1,0:T(4,128)(2,1)S(1)} %slice_bitcast_fusion.16), channel_id=1, source_target_pairs={{1,0},{2,1},{3,2},{5,4},{6,5},{7,6},{9,8},{10,9},{11,10},{13,12},{... | collective-permute-start | bytes 24584 | tf_op jit(solution)/shard_map/ppermute | solution.py:23
  87.5 6.2 %collective-permute-start.4 = (bf16[1,4,4,256]{3,2,1,0:T(4,128)(2,1)S(1)}, bf16[1,4,4,256]{3,2,1,0:T(4,128)(2,1)S(1)}, u32[]{:S(2)}, u32[]{:S(2)}) collective-permute-start(bf16[1,4,4,256]{3,2,1,0:T(4,128)(2,1)S(1)} %slice_bitcast_fusion.15), channel_id=1, source_target_pairs={{0,1},{1,2},{2,3},{4,5},{5,6},{6,7},{8,9},{9,10},{10,11},{12,13},{... | collective-permute-start | bytes 24584 | tf_op jit(solution)/shard_map/ppermute | solution.py:21
  91.8 3.1 %collective-permute-start.5 = (bf16[1,4,4,256]{3,2,1,0:T(4,128)(2,1)S(1)}, bf16[1,4,4,256]{3,2,1,0:T(4,128)(2,1)S(1)}, u32[]{:S(2)}, u32[]{:S(2)}) collective-permute-start(bf16[1,4,4,256]{3,2,1,0:T(4,128)(2,1)S(1)} %slice_bitcast_fusion.14), channel_id=1, source_target_pairs={{1,0},{2,1},{3,2},{5,4},{6,5},{7,6},{9,8},{10,9},{11,10},{13,12},{... | collective-permute-start | bytes 24584 | tf_op jit(solution)/shard_map/ppermute | solution.py:23
  106.8 5.8 %collective-permute-start.6 = (bf16[1,4,4,256]{3,2,1,0:T(4,128)(2,1)S(1)}, bf16[1,4,4,256]{3,2,1,0:T(4,128)(2,1)S(1)}, u32[]{:S(2)}, u32[]{:S(2)}) collective-permute-start(bf16[1,4,4,256]{3,2,1,0:T(4,128)(2,1)S(1)} %slice_bitcast_fusion.13), channel_id=1, source_target_pairs={{0,1},{1,2},{2,3},{4,5},{5,6},{6,7},{8,9},{9,10},{10,11},{12,13},{... | collective-permute-start | bytes 24584 | tf_op jit(solution)/shard_map/ppermute | solution.py:21
  110.7 3.1 %collective-permute-start.7 = (bf16[1,4,4,256]{3,2,1,0:T(4,128)(2,1)S(1)}, bf16[1,4,4,256]{3,2,1,0:T(4,128)(2,1)S(1)}, u32[]{:S(2)}, u32[]{:S(2)}) collective-permute-start(bf16[1,4,4,256]{3,2,1,0:T(4,128)(2,1)S(1)} %slice_bitcast_fusion.12), channel_id=1, source_target_pairs={{1,0},{2,1},{3,2},{5,4},{6,5},{7,6},{9,8},{10,9},{11,10},{13,12},{... | collective-permute-start | bytes 24584 | tf_op jit(solution)/shard_map/ppermute | solution.py:23
  134.0 9.0 %collective-permute-start.8 = (bf16[1,4,4,256]{3,2,1,0:T(4,128)(2,1)S(1)}, bf16[1,4,4,256]{3,2,1,0:T(4,128)(2,1)S(1)}, u32[]{:S(2)}, u32[]{:S(2)}) collective-permute-start(bf16[1,4,4,256]{3,2,1,0:T(4,128)(2,1)S(1)} %slice_bitcast_fusion.11), channel_id=1, source_target_pairs={{0,1},{1,2},{2,3},{4,5},{5,6},{6,7},{8,9},{9,10},{10,11},{12,13},{... | collective-permute-start | bytes 24584 | tf_op jit(solution)/shard_map/ppermute | solution.py:21
  137.8 5.2 %collective-permute-start.9 = (bf16[1,4,4,256]{3,2,1,0:T(4,128)(2,1)S(1)}, bf16[1,4,4,256]{3,2,1,0:T(4,128)(2,1)S(1)}, u32[]{:S(2)}, u32[]{:S(2)}) collective-permute-start(bf16[1,4,4,256]{3,2,1,0:T(4,128)(2,1)S(1)} %slice_bitcast_fusion.10), channel_id=1, source_target_pairs={{1,0},{2,1},{3,2},{5,4},{6,5},{7,6},{9,8},{10,9},{11,10},{13,12},{... | collective-permute-start | bytes 24584 | tf_op jit(solution)/shard_map/ppermute | solution.py:23
  139.4 115.9 %collective-permute-start.14 = (bf16[64,512]{1,0:T(8,128)(2,1)S(1)}, bf16[64,512]{1,0:T(8,128)(2,1)S(1)}, u32[]{:S(2)}, u32[]{:S(2)}) collective-permute-start(bf16[64,512]{1,0:T(8,128)(2,1)S(1)} %bitcast_convert_fusion), channel_id=1, source_target_pairs={{0,4},{4,8},{8,12},{12,16},{16,20},{20,24},{24,28},{1,5},{5,9},{9,... | collective-permute-start | bytes 196616 | tf_op jit(solution)/shard_map/ppermute | solution.py:33
  154.8 4.7 %collective-permute-start.10 = (bf16[1,4,4,256]{3,2,1,0:T(4,128)(2,1)S(1)}, bf16[1,4,4,256]{3,2,1,0:T(4,128)(2,1)S(1)}, u32[]{:S(2)}, u32[]{:S(2)}) collective-permute-start(bf16[1,4,4,256]{3,2,1,0:T(4,128)(2,1)S(1)} %slice_bitcast_fusion.9), channel_id=1, source_target_pairs={{0,1},{1,2},{2,3},{4,5},{5,6},{6,7},{8,9},{9,10},{10,11},{12,13},{... | collective-permute-start | bytes 24584 | tf_op jit(solution)/shard_map/ppermute | solution.py:21
  157.6 4.1 %collective-permute-start.11 = (bf16[1,4,4,256]{3,2,1,0:T(4,128)(2,1)S(1)}, bf16[1,4,4,256]{3,2,1,0:T(4,128)(2,1)S(1)}, u32[]{:S(2)}, u32[]{:S(2)}) collective-permute-start(bf16[1,4,4,256]{3,2,1,0:T(4,128)(2,1)S(1)} %slice_bitcast_fusion.8), channel_id=1, source_target_pairs={{1,0},{2,1},{3,2},{5,4},{6,5},{7,6},{9,8},{10,9},{11,10},{13,12},{... | collective-permute-start | bytes 24584 | tf_op jit(solution)/shard_map/ppermute | solution.py:23
  174.0 8.8 %collective-permute-start.12 = (bf16[1,4,4,256]{3,2,1,0:T(4,128)(2,1)S(1)}, bf16[1,4,4,256]{3,2,1,0:T(4,128)(2,1)S(1)}, u32[]{:S(2)}, u32[]{:S(2)}) collective-permute-start(bf16[1,4,4,256]{3,2,1,0:T(4,128)(2,1)S(1)} %slice_bitcast_fusion.7), channel_id=1, source_target_pairs={{0,1},{1,2},{2,3},{4,5},{5,6},{6,7},{8,9},{9,10},{10,11},{12,13},{... | collective-permute-start | bytes 24584 | tf_op jit(solution)/shard_map/ppermute | solution.py:21
  178.3 4.5 %collective-permute-start.13 = (bf16[1,4,4,256]{3,2,1,0:T(4,128)(2,1)S(1)}, bf16[1,4,4,256]{3,2,1,0:T(4,128)(2,1)S(1)}, u32[]{:S(2)}, u32[]{:S(2)}) collective-permute-start(bf16[1,4,4,256]{3,2,1,0:T(4,128)(2,1)S(1)} %slice_bitcast_fusion.6), channel_id=1, source_target_pairs={{1,0},{2,1},{3,2},{5,4},{6,5},{7,6},{9,8},{10,9},{11,10},{13,12},{... | collective-permute-start | bytes 24584 | tf_op jit(solution)/shard_map/ppermute | solution.py:23
  194.5 5.2 %collective-permute-start.15 = (bf16[1,4,4,256]{3,2,1,0:T(4,128)(2,1)S(1)}, bf16[1,4,4,256]{3,2,1,0:T(4,128)(2,1)S(1)}, u32[]{:S(2)}, u32[]{:S(2)}) collective-permute-start(bf16[1,4,4,256]{3,2,1,0:T(4,128)(2,1)S(1)} %slice_bitcast_fusion.5), channel_id=1, source_target_pairs={{0,1},{1,2},{2,3},{4,5},{5,6},{6,7},{8,9},{9,10},{10,11},{12,13},{... | collective-permute-start | bytes 24584 | tf_op jit(solution)/shard_map/ppermute | solution.py:21
  197.6 3.8 %collective-permute-start.16 = (bf16[1,4,4,256]{3,2,1,0:T(4,128)(2,1)S(1)}, bf16[1,4,4,256]{3,2,1,0:T(4,128)(2,1)S(1)}, u32[]{:S(2)}, u32[]{:S(2)}) collective-permute-start(bf16[1,4,4,256]{3,2,1,0:T(4,128)(2,1)S(1)} %slice_bitcast_fusion.4), channel_id=1, source_target_pairs={{1,0},{2,1},{3,2},{5,4},{6,5},{7,6},{9,8},{10,9},{11,10},{13,12},{... | collective-permute-start | bytes 24584 | tf_op jit(solution)/shard_map/ppermute | solution.py:23
  253.3 9.3 %collective-permute-start.17 = (f32[64,512]{0,1:T(8,128)S(1)}, f32[64,512]{0,1:T(8,128)S(1)}, u32[]{:S(2)}, u32[]{:S(2)}) collective-permute-start(f32[64,512]{0,1:T(8,128)S(1)} %select_bitcast_fusion.1), channel_id=1, source_target_pairs={{4,0},{8,4},{12,8},{16,12},{20,16},{24,20},{28,24},{5,1},{9,5},{13... | collective-permute-start | bytes 393224 | tf_op jit(solution)/shard_map/ppermute | solution.py:33
where the time goes:
time: 269 us; the launch traced here: 265 us
  local copies, waits for them, and re-layouts  77.5 us (29%)
  other arithmetic  76 us (28%)
  starting transfers between devices  44.9 us (17%)
  blocking collectives  41.3 us (15%)
  waiting for transfers between devices  14 us (5%)
  between operations  11 us (4%)
    unnamed x15, other arithmetic  66.5 us
    psum x1, blocking collectives, per_device(): lax.psum(local_cost, ('tm', 'space'))  41.3 us
    ppermute x8, starting transfers between devices, padded_2(): lax.ppermute(tail, axis, [(i, (i + 1) % count) for i in range(ends)])  29.6 us
    gather x9, local copies, waits for them, and re-layouts, arrange(): return jnp.take(values, inverse, axis=-1)  29.1 us
    unnamed x24, local copies, waits for them, and re-layouts  18.2 us
    ppermute x8, starting transfers between devices, padded_2(): lax.ppermute(head, axis, [((i + 1) % count, i) for i in range(ends)])  10.5 us
    ppermute x8, waiting for transfers between devices, padded_2(): lax.ppermute(head, axis, [((i + 1) % count, i) for i in range(ends)])  8.72 us
    reshape x48, local copies, waits for them, and re-layouts, fetch(): return moved.reshape(traces.shape)  7.46 us
  transfers between devices with their start and end apart: 18, of which 6 were waited for; matrix products, arithmetic and copies ran while one was open for 35% of the time, Pallas kernels for 0%

commit v1 on v0

--- a/solution.py
+++ b/solution.py
@@ -152,7 +152,7 @@
             weight = (first_step + index_k).astype(jnp.float32) / total_steps
             adjoint = weight * (before - goal) + carried
     new_controls = restore(jnp.stack(updated))
-    objective = lax.psum(local_cost, ("tm", "space")) / (
+    objective = jnp.sum(lax.all_gather(local_cost, ("tm", "space")), axis=0) / (
         total_steps * nodes * elements * lax.axis_size("space")
     )
     moved_state = from_behind(history[-1].astype(jnp.bfloat16), "tm", 1).astype(jnp.float32)

time: 269 us -> 269 us (level)
    unnamed x0 -> x1, blocking collectives: none -> 41.3 us
    psum x1 -> x0, blocking collectives: 41.3 us -> none  [per_device(): lax.psum(local_cost, ('tm', 'space'))]
    unnamed x24 -> x26, local copies, waits for them, and re-layouts: 18.2 us -> 18.3 us
where the time goes in v1:
time: 269 us; the launch traced here: 265 us
  local copies, waits for them, and re-layouts  77.7 us (29%)
  other arithmetic  76.6 us (28%)
  starting transfers between devices  44.9 us (17%)
  blocking collectives  41.3 us (15%)
  waiting for transfers between devices  13.8 us (5%)
  between operations  11 us (4%)
    unnamed x15, other arithmetic  66.5 us
    unnamed x1, blocking collectives  41.3 us
    ppermute x8, starting transfers between devices, padded_2(): lax.ppermute(tail, axis, [(i, (i + 1) % count) for i in range(ends)])  29.6 us
    gather x9, local copies, waits for them, and re-layouts, arrange(): return jnp.take(values, inverse, axis=-1)  29.1 us
    unnamed x26, local copies, waits for them, and re-layouts  18.3 us
    ppermute x8, starting transfers between devices, padded_2(): lax.ppermute(head, axis, [((i + 1) % count, i) for i in range(ends)])  10.5 us
    ppermute x8, waiting for transfers between devices, padded_2(): lax.ppermute(head, axis, [((i + 1) % count, i) for i in range(ends)])  8.72 us
    reshape x48, local copies, waits for them, and re-layouts, fetch(): return moved.reshape(traces.shape)  7.46 us
  transfers between devices with their start and end apart: 18, of which 6 were waited for; matrix products, arithmetic and copies ran while one was open for 35% of the time, Pallas kernels for 0%

profile of v1, /device:TPU:0, one launch (start us, length us, event | category | flops | bytes accessed | tf_op | source)
XLA Modules:
  0.0 265.3 jit_solution(9593343008857703814)
XLA Ops:
  1.4 2.4 scatter_custom_fusion
  6.1 2.4 collective-permute-start
  15.7 13.0 %copy.148 = bf16[64,64,512]{1,0,2:T(8,128)(2,1)} copy(bf16[64,64,512]{2,1,0:T(8,128)(2,1)} %param.110) | data formatting | bytes 8388608 | tf_op args[4]
  28.8 23.0 %gather_fusion = bf16[512,64,64]{2,1,0:T(8,128)(2,1)} fusion(bf16[64,64,512]{1,0,2:T(8,128)(2,1)} %copy.148, s32[1024]{0:T(1024)S(1)} %pad_clamp_fusion.1), kind=kCustom, calls=%fused_computation.6 | custom fusion | bytes 8390656 | tf_op jit(solution)/shard_map/jit(_take)/gather | solution.py:80
  55.7 8.3 %fusion = f32[512,64]{1,0:T(8,128)S(1)} fusion(f32[512,64]{1,0:T(8,128)S(1)} %copy.235, bf16[512,64,64]{2,1,0:T(8,128)(2,1)} %gather_fusion, pred[512]{0:T(512)(128)(4,1)S(1)} %compare_and_fusion.1), kind=kLoop, calls=%fused_computation.17 | loop fusion | flops 8355840 | bytes 4456960
  66.5 5.1 %collective-permute-start.2 = (bf16[1,4,4,256]{3,2,1,0:T(4,128)(2,1)S(1)}, bf16[1,4,4,256]{3,2,1,0:T(4,128)(2,1)S(1)}, u32[]{:S(2)}, u32[]{:S(2)}) collective-permute-start(bf16[1,4,4,256]{3,2,1,0:T(4,128)(2,1)S(1)} %slice_bitcast_fusion.17), channel_id=1, source_target_pairs={{0,1},{1,2},{2,3},{4,5},{5,6},{6,7},{8,9},{9,10},{10,11},{12,13},{... | collective-permute-start | bytes 24584 | tf_op jit(solution)/shard_map/ppermute | solution.py:21
  73.6 2.4 collective-permute-done.3
  76.9 8.1 %fusion.1 = f32[512,64]{1,0:T(8,128)S(1)} fusion(f32[512,64]{1,0:T(8,128)S(1)} %copy.236, bf16[512,64,64]{2,1,0:T(8,128)(2,1)} %gather_fusion, pred[512]{0:T(512)(128)(4,1)S(1)} %compare_and_fusion.1), kind=kLoop, calls=%fused_computation.18 | loop fusion | flops 8355840 | bytes 4456960
  87.5 4.3 %collective-permute-start.4 = (bf16[1,4,4,256]{3,2,1,0:T(4,128)(2,1)S(1)}, bf16[1,4,4,256]{3,2,1,0:T(4,128)(2,1)S(1)}, u32[]{:S(2)}, u32[]{:S(2)}) collective-permute-start(bf16[1,4,4,256]{3,2,1,0:T(4,128)(2,1)S(1)} %slice_bitcast_fusion.15), channel_id=1, source_target_pairs={{0,1},{1,2},{2,3},{4,5},{5,6},{6,7},{8,9},{9,10},{10,11},{12,13},{... | collective-permute-start | bytes 24584 | tf_op jit(solution)/shard_map/ppermute | solution.py:21
  95.8 8.5 %fusion.2 = f32[512,64]{1,0:T(8,128)S(1)} fusion(f32[512,64]{1,0:T(8,128)S(1)} %copy.237, bf16[512,64,64]{2,1,0:T(8,128)(2,1)} %gather_fusion, pred[512]{0:T(512)(128)(4,1)S(1)} %compare_and_fusion.1), kind=kLoop, calls=%fused_computation.19 | loop fusion | flops 8355840 | bytes 4456960
  106.8 3.8 %collective-permute-start.6 = (bf16[1,4,4,256]{3,2,1,0:T(4,128)(2,1)S(1)}, bf16[1,4,4,256]{3,2,1,0:T(4,128)(2,1)S(1)}, u32[]{:S(2)}, u32[]{:S(2)}) collective-permute-start(bf16[1,4,4,256]{3,2,1,0:T(4,128)(2,1)S(1)} %slice_bitcast_fusion.13), channel_id=1, source_target_pairs={{0,1},{1,2},{2,3},{4,5},{5,6},{6,7},{8,9},{9,10},{10,11},{12,13},{... | collective-permute-start | bytes 24584 | tf_op jit(solution)/shard_map/ppermute | solution.py:21
  114.7 8.1 %fusion.3 = f32[512,64]{1,0:T(8,128)S(1)} fusion(f32[512,64]{1,0:T(8,128)S(1)} %copy.238, bf16[512,64,64]{2,1,0:T(8,128)(2,1)} %gather_fusion, pred[512]{0:T(512)(128)(4,1)S(1)} %compare_and_fusion.1), kind=kLoop, calls=%fused_computation.20 | loop fusion | flops 8355840 | bytes 4456960
  123.1 8.2 %fusion.4 = f32[512,64]{1,0:T(8,128)S(1)} fusion(f32[512,64]{1,0:T(8,128)S(1)} %copy.239, bf16[512,64,64]{2,1,0:T(8,128)(2,1)} %gather_fusion, pred[512]{0:T(512)(128)(4,1)S(1)} %compare_and_fusion.1), kind=kLoop, calls=%fused_computation.21 | loop fusion | flops 8355840 | bytes 4456960
  134.0 3.8 %collective-permute-start.8 = (bf16[1,4,4,256]{3,2,1,0:T(4,128)(2,1)S(1)}, bf16[1,4,4,256]{3,2,1,0:T(4,128)(2,1)S(1)}, u32[]{:S(2)}, u32[]{:S(2)}) collective-permute-start(bf16[1,4,4,256]{3,2,1,0:T(4,128)(2,1)S(1)} %slice_bitcast_fusion.11), channel_id=1, source_target_pairs={{0,1},{1,2},{2,3},{4,5},{5,6},{6,7},{8,9},{9,10},{10,11},{12,13},{... | collective-permute-start | bytes 24584 | tf_op jit(solution)/shard_map/ppermute | solution.py:21
  139.4 3.4 %collective-permute-start.14 = (bf16[64,512]{1,0:T(8,128)(2,1)S(1)}, bf16[64,512]{1,0:T(8,128)(2,1)S(1)}, u32[]{:S(2)}, u32[]{:S(2)}) collective-permute-start(bf16[64,512]{1,0:T(8,128)(2,1)S(1)} %bitcast_convert_fusion), channel_id=1, source_target_pairs={{0,4},{4,8},{8,12},{12,16},{16,20},{20,24},{24,28},{1,5},{5,9},{9,... | collective-permute-start | bytes 196616 | tf_op jit(solution)/shard_map/ppermute | solution.py:33
  144.0 8.4 %fusion.5 = f32[512,64]{1,0:T(8,128)S(1)} fusion(f32[512,64]{1,0:T(8,128)S(1)} %copy.240, bf16[512,64,64]{2,1,0:T(8,128)(2,1)} %gather_fusion, pred[512]{0:T(512)(128)(4,1)S(1)} %compare_and_fusion.1), kind=kLoop, calls=%fused_computation.22 | loop fusion | flops 8355840 | bytes 4456960
  154.9 2.8 %collective-permute-start.10 = (bf16[1,4,4,256]{3,2,1,0:T(4,128)(2,1)S(1)}, bf16[1,4,4,256]{3,2,1,0:T(4,128)(2,1)S(1)}, u32[]{:S(2)}, u32[]{:S(2)}) collective-permute-start(bf16[1,4,4,256]{3,2,1,0:T(4,128)(2,1)S(1)} %slice_bitcast_fusion.9), channel_id=1, source_target_pairs={{0,1},{1,2},{2,3},{4,5},{5,6},{6,7},{8,9},{9,10},{10,11},{12,13},{... | collective-permute-start | bytes 24584 | tf_op jit(solution)/shard_map/ppermute | solution.py:21
  159.5 2.2 collective-permute-done.11
  163.4 8.2 %fusion.6 = f32[512,64]{1,0:T(8,128)S(1)} fusion(f32[512,64]{1,0:T(8,128)S(1)} %copy.241, bf16[512,64,64]{2,1,0:T(8,128)(2,1)} %gather_fusion, pred[512]{0:T(512)(128)(4,1)S(1)} %compare_and_fusion.1), kind=kLoop, calls=%fused_computation.23 | loop fusion | flops 8355840 | bytes 4456960
  174.0 4.3 %collective-permute-start.12 = (bf16[1,4,4,256]{3,2,1,0:T(4,128)(2,1)S(1)}, bf16[1,4,4,256]{3,2,1,0:T(4,128)(2,1)S(1)}, u32[]{:S(2)}, u32[]{:S(2)}) collective-permute-start(bf16[1,4,4,256]{3,2,1,0:T(4,128)(2,1)S(1)} %slice_bitcast_fusion.7), channel_id=1, source_target_pairs={{0,1},{1,2},{2,3},{4,5},{5,6},{6,7},{8,9},{9,10},{10,11},{12,13},{... | collective-permute-start | bytes 24584 | tf_op jit(solution)/shard_map/ppermute | solution.py:21
  183.8 8.2 %fusion.7 = f32[512,64]{1,0:T(8,128)S(1)} fusion(f32[512,64]{1,0:T(8,128)S(1)} %copy.242, bf16[512,64,64]{2,1,0:T(8,128)(2,1)} %gather_fusion, pred[512]{0:T(512)(128)(4,1)S(1)} %compare_and_fusion.1), kind=kLoop, calls=%fused_computation.24 | loop fusion | flops 8355840 | bytes 4456960
  194.5 3.0 %collective-permute-start.15 = (bf16[1,4,4,256]{3,2,1,0:T(4,128)(2,1)S(1)}, bf16[1,4,4,256]{3,2,1,0:T(4,128)(2,1)S(1)}, u32[]{:S(2)}, u32[]{:S(2)}) collective-permute-start(bf16[1,4,4,256]{3,2,1,0:T(4,128)(2,1)S(1)} %slice_bitcast_fusion.5), channel_id=1, source_target_pairs={{0,1},{1,2},{2,3},{4,5},{5,6},{6,7},{8,9},{9,10},{10,11},{12,13},{... | collective-permute-start | bytes 24584 | tf_op jit(solution)/shard_map/ppermute | solution.py:21
  211.1 41.3 %all-reduce.8 = f32[32]{0:T(128)S(1)} all-reduce(f32[32]{0:T(128)S(1)} %dynamic-update-slice.144), channel_id=1, replica_groups=mesh['tm'=8,'space'=4] {'tm','space'}, use_global_device_ids=true, to_apply=%add.8 | all-reduce | flops 32 | bytes 256
  258.1 5.1 %collective-permute-done.17 = f32[64,512]{0,1:T(8,128)S(1)} collective-permute-done((f32[64,512]{0,1:T(8,128)S(1)}, f32[64,512]{0,1:T(8,128)S(1)}, u32[]{:S(2)}, u32[]{:S(2)}) %collective-permute-start.17) | collective-permute-done | bytes 131104 | tf_op jit(solution)/shard_map/ppermute | solution.py:33
  (480 shorter events, 65.5 us)
Async XLA Ops:
  0.6 11.7 %copy-start.3 = (s32[1,512]{1,0:T(1,128)S(1)}, s32[1,512]{1,0:T(1,128)}, u32[]{:S(2)}) copy-start(s32[1,512]{1,0:T(1,128)} %param.111) | copy-start | bytes 6148
  0.6 11.9 %copy-start = (bf16[4,64,512]{2,1,0:T(8,128)(2,1)S(1)}, bf16[4,64,512]{2,1,0:T(8,128)(2,1)}, u32[]{:S(2)}) copy-start(bf16[4,64,512]{2,1,0:T(8,128)(2,1)} %param.106) | copy-start | bytes 786436
  6.1 48.6 %collective-permute-start = (bf16[1,4,4,256]{3,2,1,0:T(4,128)(2,1)S(1)}, bf16[1,4,4,256]{3,2,1,0:T(4,128)(2,1)S(1)}, u32[]{:S(2)}, u32[]{:S(2)}) collective-permute-start(bf16[1,4,4,256]{3,2,1,0:T(4,128)(2,1)S(1)} %slice_bitcast_fusion.19), channel_id=1, source_target_pairs={{0,1},{1,2},{2,3},{4,5},{5,6},{6,7},{8,9},{9,10},{10,11},{12,13},{... | collective-permute-start | bytes 24584 | tf_op jit(solution)/shard_map/ppermute | solution.py:21
  8.6 46.2 %collective-permute-start.1 = (bf16[1,4,4,256]{3,2,1,0:T(4,128)(2,1)S(1)}, bf16[1,4,4,256]{3,2,1,0:T(4,128)(2,1)S(1)}, u32[]{:S(2)}, u32[]{:S(2)}) collective-permute-start(bf16[1,4,4,256]{3,2,1,0:T(4,128)(2,1)S(1)} %slice_bitcast_fusion.18), channel_id=1, source_target_pairs={{1,0},{2,1},{3,2},{5,4},{6,5},{7,6},{9,8},{10,9},{11,10},{13,12},{... | collective-permute-start | bytes 24584 | tf_op jit(solution)/shard_map/ppermute | solution.py:23
  15.7 36.1 %copy-start.2 = (bf16[64,512]{1,0:T(8,128)(2,1)S(1)}, bf16[64,512]{1,0:T(8,128)(2,1)}, u32[]{:S(2)}) copy-start(bf16[64,512]{1,0:T(8,128)(2,1)} %param.107) | copy-start | bytes 196612
  15.7 37.7 %copy-start.1 = (f32[1,64,512]{2,1,0:T(8,128)S(1)}, f32[1,64,512]{2,1,0:T(8,128)}, u32[]{:S(2)}) copy-start(f32[1,64,512]{2,1,0:T(8,128)} %param.109) | copy-start | bytes 393220
  66.5 7.1 %collective-permute-start.2 = (bf16[1,4,4,256]{3,2,1,0:T(4,128)(2,1)S(1)}, bf16[1,4,4,256]{3,2,1,0:T(4,128)(2,1)S(1)}, u32[]{:S(2)}, u32[]{:S(2)}) collective-permute-start(bf16[1,4,4,256]{3,2,1,0:T(4,128)(2,1)S(1)} %slice_bitcast_fusion.17), channel_id=1, source_target_pairs={{0,1},{1,2},{2,3},{4,5},{5,6},{6,7},{8,9},{9,10},{10,11},{12,13},{... | collective-permute-start | bytes 24584 | tf_op jit(solution)/shard_map/ppermute | solution.py:21
  71.7 4.3 %collective-permute-start.3 = (bf16[1,4,4,256]{3,2,1,0:T(4,128)(2,1)S(1)}, bf16[1,4,4,256]{3,2,1,0:T(4,128)(2,1)S(1)}, u32[]{:S(2)}, u32[]{:S(2)}) collective-permute-start(bf16[1,4,4,256]{3,2,1,0:T(4,128)(2,1)S(1)} %slice_bitcast_fusion.16), channel_id=1, source_target_pairs={{1,0},{2,1},{3,2},{5,4},{6,5},{7,6},{9,8},{10,9},{11,10},{13,12},{... | collective-permute-start | bytes 24584 | tf_op jit(solution)/shard_map/ppermute | solution.py:23
  87.5 6.2 %collective-permute-start.4 = (bf16[1,4,4,256]{3,2,1,0:T(4,128)(2,1)S(1)}, bf16[1,4,4,256]{3,2,1,0:T(4,128)(2,1)S(1)}, u32[]{:S(2)}, u32[]{:S(2)}) collective-permute-start(bf16[1,4,4,256]{3,2,1,0:T(4,128)(2,1)S(1)} %slice_bitcast_fusion.15), channel_id=1, source_target_pairs={{0,1},{1,2},{2,3},{4,5},{5,6},{6,7},{8,9},{9,10},{10,11},{12,13},{... | collective-permute-start | bytes 24584 | tf_op jit(solution)/shard_map/ppermute | solution.py:21
  91.8 3.1 %collective-permute-start.5 = (bf16[1,4,4,256]{3,2,1,0:T(4,128)(2,1)S(1)}, bf16[1,4,4,256]{3,2,1,0:T(4,128)(2,1)S(1)}, u32[]{:S(2)}, u32[]{:S(2)}) collective-permute-start(bf16[1,4,4,256]{3,2,1,0:T(4,128)(2,1)S(1)} %slice_bitcast_fusion.14), channel_id=1, source_target_pairs={{1,0},{2,1},{3,2},{5,4},{6,5},{7,6},{9,8},{10,9},{11,10},{13,12},{... | collective-permute-start | bytes 24584 | tf_op jit(solution)/shard_map/ppermute | solution.py:23
  106.8 5.8 %collective-permute-start.6 = (bf16[1,4,4,256]{3,2,1,0:T(4,128)(2,1)S(1)}, bf16[1,4,4,256]{3,2,1,0:T(4,128)(2,1)S(1)}, u32[]{:S(2)}, u32[]{:S(2)}) collective-permute-start(bf16[1,4,4,256]{3,2,1,0:T(4,128)(2,1)S(1)} %slice_bitcast_fusion.13), channel_id=1, source_target_pairs={{0,1},{1,2},{2,3},{4,5},{5,6},{6,7},{8,9},{9,10},{10,11},{12,13},{... | collective-permute-start | bytes 24584 | tf_op jit(solution)/shard_map/ppermute | solution.py:21
  110.7 3.1 %collective-permute-start.7 = (bf16[1,4,4,256]{3,2,1,0:T(4,128)(2,1)S(1)}, bf16[1,4,4,256]{3,2,1,0:T(4,128)(2,1)S(1)}, u32[]{:S(2)}, u32[]{:S(2)}) collective-permute-start(bf16[1,4,4,256]{3,2,1,0:T(4,128)(2,1)S(1)} %slice_bitcast_fusion.12), channel_id=1, source_target_pairs={{1,0},{2,1},{3,2},{5,4},{6,5},{7,6},{9,8},{10,9},{11,10},{13,12},{... | collective-permute-start | bytes 24584 | tf_op jit(solution)/shard_map/ppermute | solution.py:23
  134.0 9.0 %collective-permute-start.8 = (bf16[1,4,4,256]{3,2,1,0:T(4,128)(2,1)S(1)}, bf16[1,4,4,256]{3,2,1,0:T(4,128)(2,1)S(1)}, u32[]{:S(2)}, u32[]{:S(2)}) collective-permute-start(bf16[1,4,4,256]{3,2,1,0:T(4,128)(2,1)S(1)} %slice_bitcast_fusion.11), channel_id=1, source_target_pairs={{0,1},{1,2},{2,3},{4,5},{5,6},{6,7},{8,9},{9,10},{10,11},{12,13},{... | collective-permute-start | bytes 24584 | tf_op jit(solution)/shard_map/ppermute | solution.py:21
  137.9 5.2 %collective-permute-start.9 = (bf16[1,4,4,256]{3,2,1,0:T(4,128)(2,1)S(1)}, bf16[1,4,4,256]{3,2,1,0:T(4,128)(2,1)S(1)}, u32[]{:S(2)}, u32[]{:S(2)}) collective-permute-start(bf16[1,4,4,256]{3,2,1,0:T(4,128)(2,1)S(1)} %slice_bitcast_fusion.10), channel_id=1, source_target_pairs={{1,0},{2,1},{3,2},{5,4},{6,5},{7,6},{9,8},{10,9},{11,10},{13,12},{... | collective-permute-start | bytes 24584 | tf_op jit(solution)/shard_map/ppermute | solution.py:23
  139.4 116.6 %collective-permute-start.14 = (bf16[64,512]{1,0:T(8,128)(2,1)S(1)}, bf16[64,512]{1,0:T(8,128)(2,1)S(1)}, u32[]{:S(2)}, u32[]{:S(2)}) collective-permute-start(bf16[64,512]{1,0:T(8,128)(2,1)S(1)} %bitcast_convert_fusion), channel_id=1, source_target_pairs={{0,4},{4,8},{8,12},{12,16},{16,20},{20,24},{24,28},{1,5},{5,9},{9,... | collective-permute-start | bytes 196616 | tf_op jit(solution)/shard_map/ppermute | solution.py:33
  154.9 4.7 %collective-permute-start.10 = (bf16[1,4,4,256]{3,2,1,0:T(4,128)(2,1)S(1)}, bf16[1,4,4,256]{3,2,1,0:T(4,128)(2,1)S(1)}, u32[]{:S(2)}, u32[]{:S(2)}) collective-permute-start(bf16[1,4,4,256]{3,2,1,0:T(4,128)(2,1)S(1)} %slice_bitcast_fusion.9), channel_id=1, source_target_pairs={{0,1},{1,2},{2,3},{4,5},{5,6},{6,7},{8,9},{9,10},{10,11},{12,13},{... | collective-permute-start | bytes 24584 | tf_op jit(solution)/shard_map/ppermute | solution.py:21
  157.6 4.1 %collective-permute-start.11 = (bf16[1,4,4,256]{3,2,1,0:T(4,128)(2,1)S(1)}, bf16[1,4,4,256]{3,2,1,0:T(4,128)(2,1)S(1)}, u32[]{:S(2)}, u32[]{:S(2)}) collective-permute-start(bf16[1,4,4,256]{3,2,1,0:T(4,128)(2,1)S(1)} %slice_bitcast_fusion.8), channel_id=1, source_target_pairs={{1,0},{2,1},{3,2},{5,4},{6,5},{7,6},{9,8},{10,9},{11,10},{13,12},{... | collective-permute-start | bytes 24584 | tf_op jit(solution)/shard_map/ppermute | solution.py:23
  174.0 8.8 %collective-permute-start.12 = (bf16[1,4,4,256]{3,2,1,0:T(4,128)(2,1)S(1)}, bf16[1,4,4,256]{3,2,1,0:T(4,128)(2,1)S(1)}, u32[]{:S(2)}, u32[]{:S(2)}) collective-permute-start(bf16[1,4,4,256]{3,2,1,0:T(4,128)(2,1)S(1)} %slice_bitcast_fusion.7), channel_id=1, source_target_pairs={{0,1},{1,2},{2,3},{4,5},{5,6},{6,7},{8,9},{9,10},{10,11},{12,13},{... | collective-permute-start | bytes 24584 | tf_op jit(solution)/shard_map/ppermute | solution.py:21
  178.4 4.5 %collective-permute-start.13 = (bf16[1,4,4,256]{3,2,1,0:T(4,128)(2,1)S(1)}, bf16[1,4,4,256]{3,2,1,0:T(4,128)(2,1)S(1)}, u32[]{:S(2)}, u32[]{:S(2)}) collective-permute-start(bf16[1,4,4,256]{3,2,1,0:T(4,128)(2,1)S(1)} %slice_bitcast_fusion.6), channel_id=1, source_target_pairs={{1,0},{2,1},{3,2},{5,4},{6,5},{7,6},{9,8},{10,9},{11,10},{13,12},{... | collective-permute-start | bytes 24584 | tf_op jit(solution)/shard_map/ppermute | solution.py:23
  194.5 5.2 %collective-permute-start.15 = (bf16[1,4,4,256]{3,2,1,0:T(4,128)(2,1)S(1)}, bf16[1,4,4,256]{3,2,1,0:T(4,128)(2,1)S(1)}, u32[]{:S(2)}, u32[]{:S(2)}) collective-permute-start(bf16[1,4,4,256]{3,2,1,0:T(4,128)(2,1)S(1)} %slice_bitcast_fusion.5), channel_id=1, source_target_pairs={{0,1},{1,2},{2,3},{4,5},{5,6},{6,7},{8,9},{9,10},{10,11},{12,13},{... | collective-permute-start | bytes 24584 | tf_op jit(solution)/shard_map/ppermute | solution.py:21
  197.6 3.8 %collective-permute-start.16 = (bf16[1,4,4,256]{3,2,1,0:T(4,128)(2,1)S(1)}, bf16[1,4,4,256]{3,2,1,0:T(4,128)(2,1)S(1)}, u32[]{:S(2)}, u32[]{:S(2)}) collective-permute-start(bf16[1,4,4,256]{3,2,1,0:T(4,128)(2,1)S(1)} %slice_bitcast_fusion.4), channel_id=1, source_target_pairs={{1,0},{2,1},{3,2},{5,4},{6,5},{7,6},{9,8},{10,9},{11,10},{13,12},{... | collective-permute-start | bytes 24584 | tf_op jit(solution)/shard_map/ppermute | solution.py:23
  254.1 9.1 %collective-permute-start.17 = (f32[64,512]{0,1:T(8,128)S(1)}, f32[64,512]{0,1:T(8,128)S(1)}, u32[]{:S(2)}, u32[]{:S(2)}) collective-permute-start(f32[64,512]{0,1:T(8,128)S(1)} %select_bitcast_fusion.1), channel_id=1, source_target_pairs={{4,0},{8,4},{12,8},{16,12},{20,16},{24,20},{28,24},{5,1},{9,5},{13... | collective-permute-start | bytes 393224 | tf_op jit(solution)/shard_map/ppermute | solution.py:33
